TPU v7x, 32 devices: a whole 2x2x4 slice. The times are simulated.
32 devices in a mesh: row: 4 (over x, core), col: 8 (over z, y).
Axes of the slice: x: 2, y: 2, z: 4, core: 2. Of those that a mesh axis runs over, the one named last changes fastest.
Arguments:
- corner: bfloat16 [25600, 25600], P('row', 'col'), may hold values from -32 to 32
- edge: bfloat16 [25600, 25600], P('row', 'col'), may hold values from -32 to 32
- sketch: bfloat16 [25600, 448], P('col'), may hold values from -6 to 6
Outputs:
- corner_new: float32 [400, 400], replicated
- edge_new: float32 [400, 400], replicated
All inputs are finite; a program needn't handle non-finite values.
Results may differ from a plain program's by a relative error of at most 0.0015.
Values may be sent and summed in bfloat16 or wider, within the bound.
A program may use at most 256 MiB of HBM per device.

v0:
```python
import jax
import jax.numpy as jnp
from jax import lax
from jax.sharding import PartitionSpec as P

RANK = 400
HIGHEST = lax.Precision.HIGHEST


def outer(left, right):
    return lax.dot_general(
        left, right, (((0,), (0,)), ((), ())), preferred_element_type=jnp.float32
    )


def exact_left(rows, image):
    upper_part = image.astype(jnp.bfloat16)
    lower_part = (image - upper_part.astype(jnp.float32)).astype(jnp.bfloat16)
    return outer(rows, upper_part) + outer(rows, lower_part)


def inverse_factor(gram):
    lower = jnp.linalg.cholesky(gram)
    unit = jnp.eye(gram.shape[0], dtype=gram.dtype)
    inverse = lax.linalg.triangular_solve(lower, unit, left_side=True, lower=True)
    return inverse[gram.shape[0] - RANK :]


def column_route(n_row, n_col):
    ratio = n_col // n_row
    route = []
    for source in range(n_row):
        for shard in range(n_col):
            half, target = divmod(shard, n_row)
            route.append((source * n_col + shard, target * n_col + source * ratio + half))
    return route


def body(corner, edge, sketch):
    n_row, n_col = (lax.axis_size("row"), lax.axis_size("col"))
    both = ("row", "col")
    part = jnp.dot(corner, sketch, preferred_element_type=jnp.float32).astype(jnp.bfloat16)
    shard = lax.psum_scatter(part, "col", scatter_dimension=0, tiled=True)
    gram = lax.psum(outer(shard, shard), both)
    moved = lax.ppermute(shard, both, column_route(n_row, n_col))
    cols = lax.all_gather(moved, "row", axis=0, tiled=True)
    rows = lax.all_gather(shard, "col", axis=0, tiled=True)
    inverse = inverse_factor(gram)

    def renormalize(matrix):
        image = jnp.dot(matrix, cols, preferred_element_type=jnp.float32)
        total = exact_left(rows, image)
        half = jnp.dot(inverse, total, precision=HIGHEST)
        return lax.dot_general(half, inverse, (((1,), (1,)), ((), ())), precision=HIGHEST)

    return lax.psum((renormalize(corner), renormalize(edge)), both)


def solution(mesh):
    placed = (P("row", "col"), P("row", "col"), P("col", None))
    return jax.shard_map(body, mesh=mesh, in_specs=placed, out_specs=(P(), P()), check_vma=False)
```

profile of v0, /device:TPU:0, one launch (start us, length us, event | category | flops | bytes accessed | tf_op | source)
XLA Modules:
  0.0 720.3 jit_solution(4127353241187174518)
XLA Ops:
  7.2 1.8 copy-done
  9.0 27.6 %convolution_convert_fusion = bf16[6400,448]{0,1:T(8,128)(2,1)} fusion(bf16[6400,3200]{1,0:T(8,128)(2,1)} %param.3, bf16[3200,448]{0,1:T(8,128)(2,1)S(1)} %copy-done), kind=kOutput, calls=%fused_computation.8 | convolution fusion | flops 18352947200 | bytes 49561600 | tf_op jit(solution)/shard_map/dot_general | solution.py:42
  36.5 9.2 %copy.22 = bf16[6400,448]{1,0:T(8,128)(2,1)} copy(bf16[6400,448]{0,1:T(8,128)(2,1)} %convolution_convert_fusion) | data formatting | bytes 11468800
  45.9 124.6 %reduce-scatter.4.cloned.1.call-done = bf16[800,448]{1,0:T(8,128)(2,1)} async-done(((bf16[6400,448]{1,0:T(8,128)(2,1)}), bf16[800,448]{1,0:T(8,128)(2,1)}) %reduce-scatter.4.cloned.1.call-update) | async-done | bytes 716816
  170.5 1.7 copy.23
  172.2 0.7 collective-permute-start
  172.9 3.1 fusion.59
  176.1 0.9 copy-done.8
  177.3 0.3 all-gather.5.cloned.1.call-update
  177.6 0.3 all-reduce.9.cloned.1.call-start
  177.9 137.3 %all-reduce.7.cloned.1.call-done = f32[448,448]{0,1:T(8,128)} async-done(((f32[448,448]{0,1:T(8,128)}), f32[448,448]{0,1:T(8,128)}) %all-reduce.7.cloned.1.call-update) | async-done | bytes 802832 | tf_op jit(solution)/shard_map/psum | solution.py:44
  315.1 1.5 copy.14
  316.6 1.4 fusion.14
  318.0 0.9 copy-done.7
  319.0 11.7 %cholesky.105 = f32[128,128]{1,0:T(8,128)S(1)} custom-call(f32[128,128]{1,0:T(8,128)S(1)} %cholesky.272), custom_call_target="Cholesky" | custom-call | tf_op jit(solution)/shard_map/jit(cholesky)/cholesky | solution.py:23
  330.8 9.8 %custom-call.30 = f32[1,128,128]{1,2,0:T(8,128)S(1)} custom-call(f32[1,128,128]{2,1,0:T(8,128)S(1)} %get-tuple-element.29), custom_call_target="InvertDiagBlocksLowerTriangular" | custom-call | tf_op jit(solution)/shard_map/jit(cholesky)/cholesky | solution.py:23
  340.6 1.2 constant_dynamic-update-slice_fusion.3
  341.8 1.2 convolution_subtract_fusion.3
  343.1 11.7 %cholesky.219 = f32[128,128]{1,0:T(8,128)S(1)} custom-call(f32[128,128]{1,0:T(8,128)S(1)} %cholesky.276), custom_call_target="Cholesky" | custom-call | tf_op jit(solution)/shard_map/jit(cholesky)/cholesky | solution.py:23
  354.8 10.2 %custom-call.31 = f32[1,128,128]{1,2,0:T(8,128)S(1)} custom-call(f32[1,128,128]{2,1,0:T(8,128)S(1)} %get-tuple-element.26), custom_call_target="InvertDiagBlocksLowerTriangular" | custom-call | tf_op jit(solution)/shard_map/jit(cholesky)/cholesky | solution.py:23
  365.0 0.2 convolution_dynamic-update-slice_fusion
  365.3 1.2 convolution_subtract_fusion.4
  366.5 11.7 %cholesky.240 = f32[128,128]{1,0:T(8,128)S(1)} custom-call(f32[128,128]{1,0:T(8,128)S(1)} %cholesky.281), custom_call_target="Cholesky" | custom-call | tf_op jit(solution)/shard_map/jit(cholesky)/cholesky | solution.py:23
  378.2 9.8 %custom-call.32 = f32[1,128,128]{1,2,0:T(8,128)S(1)} custom-call(f32[1,128,128]{2,1,0:T(8,128)S(1)} %get-tuple-element.23), custom_call_target="InvertDiagBlocksLowerTriangular" | custom-call | tf_op jit(solution)/shard_map/jit(cholesky)/cholesky | solution.py:23
  388.1 0.2 convolution_dynamic-update-slice_fusion.1
  388.3 1.0 convolution_subtract_fusion.5
  389.3 0.7 compare_reduce_fusion.2
  389.9 5.8 cholesky.260
  397.0 0.7 compare_reduce_fusion.1
  398.4 0.7 compare_reduce_fusion
  399.7 0.1 select_select_fusion
  399.9 0.8 copy-done.6
  400.7 9.0 %while.1 = (s32[]{:T(128)}, f32[448,448]{1,0:T(8,128)}, s32[3,2]{0,1:T(2,128)S(1)}, f32[3,128,128]{2,1,0:T(8,128)S(1)}, s32[]{:T(128)}) while((s32[]{:T(128)}, f32[448,448]{1,0:T(8,128)}, s32[3,2]{0,1:T(2,128)S(1)}, f32[3,128,128]{2,1,0:T(8,128)S(1)}, s32[]{:T(128)}) %tuple.46), condition=%wide.while_cond, body=%wide.while_body.sunk | while | flops 2 | bytes 131189 | solution.py:25
  401.0 0.6 fusion.88
  401.6 2.3 bitcast_dynamic-update-slice_fusion.2
  403.9 0.6 fusion.88
  404.5 2.3 bitcast_dynamic-update-slice_fusion.2
  406.9 0.6 fusion.88
  407.5 2.3 bitcast_dynamic-update-slice_fusion.2
  409.8 39.3 %custom-call.33 = f32[4,128,128]{1,2,0:T(8,128)S(1)} custom-call(f32[4,128,128]{2,1,0:T(8,128)S(1)} %pad_maximum_fusion.3), custom_call_target="InvertDiagBlocksLowerTriangular" | custom-call | tf_op jit(solution)/shard_map/triangular_solve | solution.py:25
  449.1 0.2 fusion.24
  449.4 1.2 convolution_subtract_fusion.2
  450.6 0.3 fusion.36
  450.9 1.4 convolution_subtract_fusion.1
  452.4 0.3 fusion.34
  452.7 1.6 convolution_subtract_fusion
  454.3 0.3 fusion.42
  454.7 6.2 copy.18
  460.9 6.3 reshape.63
  467.1 28.6 %fusion.60 = f32[448,6400]{1,0:T(8,128)} fusion(bf16[3200,448]{0,1:T(8,128)(2,1)} %reshape.63, bf16[6400,3200]{1,0:T(8,128)(2,1)} %param.3), kind=kOutput, calls=%fused_computation.100 | convolution fusion | flops 18350080000 | bytes 55296000 | tf_op jit(solution)/shard_map/dot_general | solution.py:51
  495.7 28.9 %fusion.61 = f32[448,6400]{1,0:T(8,128)} fusion(bf16[3200,448]{0,1:T(8,128)(2,1)} %reshape.63, bf16[6400,3200]{1,0:T(8,128)(2,1)} %param.4), kind=kOutput, calls=%fused_computation.101 | convolution fusion | flops 18350080000 | bytes 55296000 | tf_op jit(solution)/shard_map/dot_general | solution.py:51
  524.6 9.2 %copy.17 = bf16[8,800,448]{1,0,2:T(8,128)(2,1)} copy(bf16[8,800,448]{1,2,0:T(8,128)(2,1)} %all-gather.5.cloned.1.call-done) | data formatting | bytes 11468800 | tf_op jit(solution)/shard_map/all_gather | solution.py:47
  533.8 11.2 %reshape.61 = bf16[6400,448]{0,1:T(8,128)(2,1)} reshape(bf16[8,800,448]{1,0,2:T(8,128)(2,1)} %copy.17) | data formatting | bytes 11468800
  545.0 8.9 %fusion.55 = f32[448,448]{1,0:T(8,128)S(1)} fusion(bf16[6400,448]{0,1:T(8,128)(2,1)} %reshape.61, f32[448,6400]{1,0:T(8,128)} %fusion.60), kind=kOutput, calls=%fused_computation.97 | convolution fusion | flops 2569011200 | bytes 18006016 | tf_op jit(solution)/shard_map/dot_general | solution.py:11
  553.9 6.7 fusion.11
  560.6 2.5 fusion.48
  563.1 2.7 fusion.47
  565.8 3.1 fusion.53
  569.0 3.1 fusion.8
  572.2 2.5 fusion.46
  574.7 2.7 fusion.49
  577.4 131.7 %all-reduce.9.cloned.1.call-done = (f32[400,400]{1,0:T(8,128)}, f32[400,400]{1,0:T(8,128)}) async-done(((f32[400,400]{1,0:T(8,128)}, f32[400,400]{1,0:T(8,128)}), (f32[400,400]{1,0:T(8,128)}, f32[400,400]{1,0:T(8,128)})) %all-reduce.9.cloned.1.call-update) | async-done | bytes 1280016 | tf_op jit(solution)/shard_map/psum | solution.py:56
  709.1 2.1 copy.43
  711.2 2.1 copy.44
  (53 shorter events, 1.1 us)
Async XLA Ops:
  7.2 1.8 copy-start
  7.2 163.3 %reduce-scatter.4.cloned.1.call-start = ((), (), s32[]{:S(2)}) async-start(), calls=%async_computation.4 | async-start | bytes 7372800
  45.8 269.3 %all-reduce.7.cloned.1.call-start = ((), (), s32[]{:S(2)}) async-start(), calls=%async_computation.1 | async-start | bytes 1835008 | tf_op jit(solution)/shard_map/psum | solution.py:44
  172.2 5.1 copy-start.5
  172.2 3.9 collective-permute-start
  176.0 278.6 %all-gather.7.cloned.1.call-start = ((), (), s32[]{:S(2)}) async-start(), calls=%async_computation.3 | async-start | bytes 4014080 | tf_op jit(solution)/shard_map/all_gather | solution.py:46
  176.1 0.9 copy-start.8
  177.0 347.6 %all-gather.5.cloned.1.call-start = ((), (), s32[]{:S(2)}) async-start(), calls=%async_computation.2 | async-start | bytes 7225344 | tf_op jit(solution)/shard_map/all_gather | solution.py:47
  177.6 531.5 %all-reduce.9.cloned.1.call-start = ((), (), s32[]{:S(2)}) async-start(), calls=%async_computation.5 | async-start | bytes 3276800 | tf_op jit(solution)/shard_map/psum | solution.py:56
  318.0 0.9 copy-start.7
  399.8 0.9 copy-start.6
  454.7 108.5 %copy-start.2 = (f32[64,448]{0,1:T(8,128)}, f32[64,448]{0,1:T(8,128)S(1)}, u32[]{:S(2)}) copy-start(f32[64,448]{0,1:T(8,128)S(1)} %fusion.42) | copy-start | bytes 344068
  545.0 8.9 %copy-start.4 = (bf16[6400,448]{0,1:T(8,128)(2,1)S(1)}, bf16[6400,448]{0,1:T(8,128)(2,1)}, u32[]{:S(2)}) copy-start(bf16[6400,448]{0,1:T(8,128)(2,1)} %reshape.61) | copy-start | bytes 17203204
  545.0 20.8 %slice-start = ((s8[11468800]{0:T(1024)(128)(4,1)}), s8[4194304]{0:T(1024)(128)(4,1)S(1)}, s32[]{:S(2)}) async-start(s8[11468800]{0:T(1024)(128)(4,1)} %bitcast.121), calls=%async_computation.6 | async-start | bytes 8388608
  545.0 20.8 %slice-start.1 = ((s8[11468800]{0:T(1024)(128)(4,1)}), s8[4194304]{0:T(1024)(128)(4,1)S(1)}, s32[]{:S(2)}) async-start(s8[11468800]{0:T(1024)(128)(4,1)} %bitcast.121), calls=%async_computation.7 | async-start | bytes 8388608
  553.9 11.9 %slice-start.2 = ((s8[11468800]{0:T(1024)(128)(4,1)}), s8[3080192]{0:T(1024)(128)(4,1)S(1)}, s32[]{:S(2)}) async-start(s8[11468800]{0:T(1024)(128)(4,1)} %bitcast.121), calls=%async_computation.8 | async-start | bytes 6160384
  569.0 3.2 copy-start.3
  569.0 144.3 %copy-start.1 = (bf16[3200,448]{0,1:T(8,128)(2,1)S(1)}, bf16[3200,448]{0,1:T(8,128)(2,1)}, u32[]{:S(2)}) copy-start(bf16[3200,448]{0,1:T(8,128)(2,1)} %param.5) | copy-start | bytes 8601604
Sparse Core Ops, SparseCore 0:
  45.9 124.5 reduce-scatter.3
  176.2 138.9 all-reduce.6
  317.3 27.8 all-gather.6
  347.8 101.0 all-gather.4
  577.5 131.5 all-reduce.8
where the time goes:
time: 726 us; the launch traced here: 720 us
  waiting for transfers between devices  394 us (54%)
  matrix products  131 us (18%)
  other arithmetic  114 us (16%)
  local copies, waits for them, and re-layouts  62.8 us (9%)
  between operations  17.2 us (2%)
    psum x1, waiting for transfers between devices, body(): gram = lax.psum(outer(shard, shard), both)  137 us
    psum x1, waiting for transfers between devices, body(): return lax.psum((renormalize(corner), renormalize(edge)), both)  132 us
    unnamed x6, waiting for transfers between devices  125 us
    another operation x14, other arithmetic, inverse_factor(): lower = jnp.linalg.cholesky(gram)  72.9 us
    dot_general x2, matrix products, renormalize(): image = jnp.dot(matrix, cols, preferred_element_type=jnp.float32)  57.5 us
    another operation x7, other arithmetic, inverse_factor(): lax.linalg.triangular_solve(lower, unit, left_side=True, lower=True)  39.5 us
    unnamed x30, local copies, waits for them, and re-layouts  37.1 us
    dot_general x1, matrix products, body(): jnp.dot(corner, sketch, preferred_element_type=jnp.float32)  27.6 us
  transfers between devices with their start and end apart: 6, of which 3 were waited for; matrix products, arithmetic and copies ran while one was open for 29% of the time, Pallas kernels for 0%

commit v1 on v0

--- a/solution.py
+++ b/solution.py
@@ -41,7 +41,9 @@
     both = ("row", "col")
     part = jnp.dot(corner, sketch, preferred_element_type=jnp.float32).astype(jnp.bfloat16)
     shard = lax.psum_scatter(part, "col", scatter_dimension=0, tiled=True)
-    gram = lax.psum(outer(shard, shard), both)
+    own = outer(shard, shard)
+    parts = lax.all_gather(own, both, axis=0, tiled=False)
+    gram = parts.sum(axis=0)
     moved = lax.ppermute(shard, both, column_route(n_row, n_col))
     cols = lax.all_gather(moved, "row", axis=0, tiled=True)
     rows = lax.all_gather(shard, "col", axis=0, tiled=True)

time: 726 us -> 823 us (1.13)
  waiting for transfers between devices: 394 us -> 480 us
  other arithmetic: 114 us -> 125 us
    psum x1 -> x0, waiting for transfers between devices: 137 us -> none  [body(): gram = lax.psum(outer(shard, shard), both)]
    all_gather x0 -> x1, waiting for transfers between devices: none -> 127 us  [body(): parts = lax.all_gather(own, both, axis=0, tiled=False)]
    all_gather x1, waiting for transfers between devices: 0.02 us -> 61.4 us  [body(): cols = lax.all_gather(moved, 'row', axis=0, tiled=True)]
    all_gather x1, waiting for transfers between devices: 0.01 us -> 35.7 us  [body(): rows = lax.all_gather(shard, 'col', axis=0, tiled=True)]
    reduce_sum x0 -> x1, other arithmetic: none -> 11.1 us  [body(): gram = parts.sum(axis=0)]
    unnamed x30 -> x26, local copies, waits for them, and re-layouts: 37.1 us -> 35.5 us
  transfers between devices with their start and end apart: 6 -> 6, of which waited for: 3 -> 5; matrix products, arithmetic and copies ran while one was open for 29% -> 15% of each run, Pallas kernels for 0% -> 0%
where the time goes in v1:
time: 823 us; the launch traced here: 815 us
  waiting for transfers between devices  480 us (58%)
  matrix products  135 us (16%)
  other arithmetic  125 us (15%)
  local copies, waits for them, and re-layouts  57.2 us (7%)
  between operations  17 us (2%)
    psum x1, waiting for transfers between devices, body(): return lax.psum((renormalize(corner), renormalize(edge)), both)  131 us
    all_gather x1, waiting for transfers between devices, body(): parts = lax.all_gather(own, both, axis=0, tiled=False)  127 us
    unnamed x6, waiting for transfers between devices  125 us
    another operation x14, other arithmetic, inverse_factor(): lower = jnp.linalg.cholesky(gram)  73 us
    all_gather x1, waiting for transfers between devices, body(): cols = lax.all_gather(moved, 'row', axis=0, tiled=True)  61.4 us
    dot_general x2, matrix products, renormalize(): image = jnp.dot(matrix, cols, preferred_element_type=jnp.float32)  55.9 us
    another operation x7, other arithmetic, inverse_factor(): lax.linalg.triangular_solve(lower, unit, left_side=True, lower=True)  39.7 us
    all_gather x1, waiting for transfers between devices, body(): rows = lax.all_gather(shard, 'col', axis=0, tiled=True)  35.7 us
  transfers between devices with their start and end apart: 6, of which 5 were waited for; matrix products, arithmetic and copies ran while one was open for 15% of the time, Pallas kernels for 0%

profile of v1, /device:TPU:0, one launch (start us, length us, event | category | flops | bytes accessed | tf_op | source)
XLA Modules:
  0.0 815.3 jit_solution(12398238981673407968)
XLA Ops:
  7.2 1.8 copy-done
  9.0 27.6 %convolution_convert_fusion = bf16[6400,448]{0,1:T(8,128)(2,1)} fusion(bf16[6400,3200]{1,0:T(8,128)(2,1)} %param.3, bf16[3200,448]{0,1:T(8,128)(2,1)S(1)} %copy-done), kind=kOutput, calls=%fused_computation.8 | convolution fusion | flops 18352947200 | bytes 49561600 | tf_op jit(solution)/shard_map/dot_general | solution.py:42
  36.6 9.1 %copy.18 = bf16[6400,448]{1,0:T(8,128)(2,1)} copy(bf16[6400,448]{0,1:T(8,128)(2,1)} %convolution_convert_fusion) | data formatting | bytes 11468800
  45.8 124.6 %reduce-scatter.4.cloned.1.call-done = bf16[800,448]{1,0:T(8,128)(2,1)} async-done(((bf16[6400,448]{1,0:T(8,128)(2,1)}), bf16[800,448]{1,0:T(8,128)(2,1)}) %reduce-scatter.4.cloned.1.call-update) | async-done | bytes 716816
  170.4 1.7 copy.19
  172.2 0.7 collective-permute-start
  172.9 0.9 copy-done.6
  173.9 0.7 all-gather.9.cloned.1.call-update
  174.6 3.0 fusion.59
  177.8 1.1 fusion.23
  178.9 61.4 %all-gather.11.cloned.1.call-done = bf16[4,800,448]{1,2,0:T(8,128)(2,1)} async-done(((bf16[1,800,448]{1,2,0:T(8,128)(2,1)}), bf16[4,800,448]{1,2,0:T(8,128)(2,1)}) %all-gather.11.cloned.1.call-update) | async-done | bytes 2867216 | tf_op jit(solution)/shard_map/all_gather | solution.py:48
  240.3 6.0 copy.15
  246.3 5.5 reshape.64
  251.8 28.0 %fusion.60 = f32[448,6400]{1,0:T(8,128)} fusion(bf16[3200,448]{0,1:T(8,128)(2,1)S(1)} %reshape.64, bf16[6400,3200]{1,0:T(8,128)(2,1)} %param.3), kind=kOutput, calls=%fused_computation.100 | convolution fusion | flops 18350080000 | bytes 55296000 | tf_op jit(solution)/shard_map/dot_general | solution.py:53
  279.9 27.8 %fusion.61 = f32[448,6400]{1,0:T(8,128)} fusion(bf16[3200,448]{0,1:T(8,128)(2,1)S(1)} %reshape.64, bf16[6400,3200]{1,0:T(8,128)(2,1)} %param.4), kind=kOutput, calls=%fused_computation.101 | convolution fusion | flops 18350080000 | bytes 55296000 | tf_op jit(solution)/shard_map/dot_general | solution.py:53
  307.7 35.7 %all-gather.9.cloned.1.call-done = bf16[8,800,448]{1,2,0:T(8,128)(2,1)} async-done(((bf16[1,800,448]{1,2,0:T(8,128)(2,1)}), bf16[8,800,448]{1,2,0:T(8,128)(2,1)}) %all-gather.9.cloned.1.call-update) | async-done | bytes 5734416 | tf_op jit(solution)/shard_map/all_gather | solution.py:49
  343.4 9.2 %copy.14 = bf16[8,800,448]{1,0,2:T(8,128)(2,1)} copy(bf16[8,800,448]{1,2,0:T(8,128)(2,1)} %all-gather.9.cloned.1.call-done) | data formatting | bytes 11468800 | tf_op jit(solution)/shard_map/all_gather | solution.py:49
  352.6 11.3 %reshape.62 = bf16[6400,448]{0,1:T(8,128)(2,1)} reshape(bf16[8,800,448]{1,0,2:T(8,128)(2,1)} %copy.14) | data formatting | bytes 11468800
  363.9 9.1 %fusion.53 = f32[448,448]{1,0:T(8,128)S(1)} fusion(bf16[6400,448]{0,1:T(8,128)(2,1)} %reshape.62, f32[448,6400]{1,0:T(8,128)} %fusion.61), kind=kOutput, calls=%fused_computation.95 | convolution fusion | flops 2569011200 | bytes 18006016 | tf_op jit(solution)/shard_map/dot_general | solution.py:11
  373.1 6.3 fusion.55
  379.4 8.0 fusion.8
  387.5 4.1 fusion.11
  391.6 126.9 %all-gather.7.cloned.1.call-done = f32[14336,448]{1,0:T(8,128)} async-done(((f32[448,448]{1,0:T(8,128)}), f32[14336,448]{1,0:T(8,128)}) %all-gather.7.cloned.1.call-update) | async-done | bytes 25690128 | tf_op jit(solution)/shard_map/all_gather | solution.py:45
  518.5 11.1 %reduce_sum.9 = f32[448,448]{1,0:T(8,128)S(1)} reduce(f32[32,448,448]{2,1,0:T(8,128)} %bitcast.120, f32[]{:T(128)} %constant.141.clone.1), dimensions={0}, to_apply=%region_1.0 | reduce | flops 6221824 | bytes 26492932 | tf_op jit(solution)/shard_map/reduce_sum | solution.py:46
  529.6 0.3 copy.11
  529.9 0.2 fusion.14
  530.1 0.9 copy-done.5
  531.0 11.7 %cholesky.105 = f32[128,128]{1,0:T(8,128)S(1)} custom-call(f32[128,128]{1,0:T(8,128)S(1)} %cholesky.272), custom_call_target="Cholesky" | custom-call | tf_op jit(solution)/shard_map/jit(cholesky)/cholesky | solution.py:23
  542.9 9.8 %custom-call.30 = f32[1,128,128]{1,2,0:T(8,128)S(1)} custom-call(f32[1,128,128]{2,1,0:T(8,128)S(1)} %get-tuple-element.29), custom_call_target="InvertDiagBlocksLowerTriangular" | custom-call | tf_op jit(solution)/shard_map/jit(cholesky)/cholesky | solution.py:23
  552.7 1.2 constant_dynamic-update-slice_fusion.3
  553.9 1.2 convolution_subtract_fusion.3
  555.2 11.7 %cholesky.219 = f32[128,128]{1,0:T(8,128)S(1)} custom-call(f32[128,128]{1,0:T(8,128)S(1)} %cholesky.276), custom_call_target="Cholesky" | custom-call | tf_op jit(solution)/shard_map/jit(cholesky)/cholesky | solution.py:23
  566.9 10.2 %custom-call.31 = f32[1,128,128]{1,2,0:T(8,128)S(1)} custom-call(f32[1,128,128]{2,1,0:T(8,128)S(1)} %get-tuple-element.26), custom_call_target="InvertDiagBlocksLowerTriangular" | custom-call | tf_op jit(solution)/shard_map/jit(cholesky)/cholesky | solution.py:23
  577.1 0.2 convolution_dynamic-update-slice_fusion
  577.4 1.2 convolution_subtract_fusion.4
  578.6 11.7 %cholesky.240 = f32[128,128]{1,0:T(8,128)S(1)} custom-call(f32[128,128]{1,0:T(8,128)S(1)} %cholesky.281), custom_call_target="Cholesky" | custom-call | tf_op jit(solution)/shard_map/jit(cholesky)/cholesky | solution.py:23
  590.3 0.7 compare_reduce_fusion.1
  591.0 9.8 %custom-call.32 = f32[1,128,128]{1,2,0:T(8,128)S(1)} custom-call(f32[1,128,128]{2,1,0:T(8,128)S(1)} %get-tuple-element.23), custom_call_target="InvertDiagBlocksLowerTriangular" | custom-call | tf_op jit(solution)/shard_map/jit(cholesky)/cholesky | solution.py:23
  601.1 1.0 convolution_subtract_fusion.5
  602.1 5.8 cholesky.260
  607.9 0.7 compare_reduce_fusion
  608.7 0.6 compare_reduce_fusion.2
  612.0 6.0 while.1
  612.1 0.5 fusion.88
  612.6 1.4 bitcast_dynamic-update-slice_fusion.2
  614.1 0.5 fusion.88
  614.6 1.4 bitcast_dynamic-update-slice_fusion.2
  616.1 0.5 fusion.88
  616.6 1.4 bitcast_dynamic-update-slice_fusion.2
  618.2 39.5 %custom-call.33 = f32[4,128,128]{1,2,0:T(8,128)S(1)} custom-call(f32[4,128,128]{2,1,0:T(8,128)S(1)} %pad_maximum_fusion.3), custom_call_target="InvertDiagBlocksLowerTriangular" | custom-call | tf_op jit(solution)/shard_map/triangular_solve | solution.py:25
  657.7 0.2 fusion.24
  657.9 0.4 convolution_subtract_fusion.2
  658.3 0.3 fusion.36
  658.6 0.5 convolution_subtract_fusion.1
  659.2 0.3 fusion.34
  659.5 0.7 convolution_subtract_fusion
  660.2 0.3 fusion.42
  660.6 3.8 fusion.46
  664.4 2.7 fusion.49
  667.1 3.7 fusion.48
  670.8 2.7 fusion.47
  673.5 130.9 %all-reduce.6.cloned.1.call-done = (f32[400,400]{1,0:T(8,128)}, f32[400,400]{1,0:T(8,128)}) async-done(((f32[400,400]{1,0:T(8,128)}, f32[400,400]{1,0:T(8,128)}), (f32[400,400]{1,0:T(8,128)}, f32[400,400]{1,0:T(8,128)})) %all-reduce.6.cloned.1.call-update) | async-done | bytes 1280016 | tf_op jit(solution)/shard_map/psum | solution.py:58
  804.4 2.1 copy.38
  806.5 2.1 copy.39
  (50 shorter events, 1.3 us)
Async XLA Ops:
  7.2 1.8 copy-start
  7.2 163.2 %reduce-scatter.4.cloned.1.call-start = ((), (), s32[]{:S(2)}) async-start(), calls=%async_computation.4 | async-start | bytes 7372800
  45.7 194.5 %all-gather.11.cloned.1.call-start = ((), (), s32[]{:S(2)}) async-start(), calls=%async_computation.3 | async-start | bytes 4014080 | tf_op jit(solution)/shard_map/all_gather | solution.py:48
  172.1 1.7 copy-start.3
  172.2 0.7 collective-permute-start
  172.9 0.9 copy-start.6
  173.8 169.6 %all-gather.9.cloned.1.call-start = ((), (), s32[]{:S(2)}) async-start(), calls=%async_computation.2 | async-start | bytes 7225344 | tf_op jit(solution)/shard_map/all_gather | solution.py:49
  174.5 343.9 %all-gather.7.cloned.1.call-start = ((), (), s32[]{:S(2)}) async-start(), calls=%async_computation.1 | async-start | bytes 30277632 | tf_op jit(solution)/shard_map/all_gather | solution.py:45
  177.6 626.8 %all-reduce.6.cloned.1.call-start = ((), (), s32[]{:S(2)}) async-start(), calls=%async_computation.5 | async-start | bytes 3276800 | tf_op jit(solution)/shard_map/psum | solution.py:58
  363.9 9.1 %copy-start.2 = (bf16[6400,448]{0,1:T(8,128)(2,1)S(1)}, bf16[6400,448]{0,1:T(8,128)(2,1)}, u32[]{:S(2)}) copy-start(bf16[6400,448]{0,1:T(8,128)(2,1)} %reshape.62) | copy-start | bytes 17203204
  373.1 14.3 %slice-start = ((s8[11468800]{0:T(1024)(128)(4,1)}), s8[4194304]{0:T(1024)(128)(4,1)S(1)}, s32[]{:S(2)}) async-start(s8[11468800]{0:T(1024)(128)(4,1)} %bitcast.123), calls=%async_computation.6 | async-start | bytes 8388608
  373.1 14.3 %slice-start.1 = ((s8[11468800]{0:T(1024)(128)(4,1)}), s8[4194304]{0:T(1024)(128)(4,1)S(1)}, s32[]{:S(2)}) async-start(s8[11468800]{0:T(1024)(128)(4,1)} %bitcast.123), calls=%async_computation.7 | async-start | bytes 8388608
  379.4 8.1 slice-start.2
  529.6 128.4 %copy-start.4 = (f32[448,448]{0,1:T(8,128)S(1)}, f32[448,448]{0,1:T(8,128)}, u32[]{:S(2)}) copy-start(f32[448,448]{0,1:T(8,128)} %fusion.23) | copy-start | bytes 2408452
  530.1 1.0 copy-start.5
  660.6 148.0 %copy-start.1 = (bf16[3200,448]{0,1:T(8,128)(2,1)S(1)}, bf16[3200,448]{0,1:T(8,128)(2,1)}, u32[]{:S(2)}) copy-start(bf16[3200,448]{0,1:T(8,128)(2,1)} %param.5) | copy-start | bytes 8601604
Sparse Core Ops, SparseCore 0:
  45.9 124.5 reduce-scatter.3
  173.9 66.3 all-gather.10
  243.0 100.2 all-gather.8
  346.1 172.2 all-gather.6
  673.6 130.7 all-reduce.5
